TPU v7x, 32 devices: a whole 2x2x4 slice. The times are simulated.
32 devices in a mesh: dp: 8 (over z, x), fsdp: 4 (over y, core).
Axes of the slice: x: 2, y: 2, z: 4, core: 2. Of those that a mesh axis runs over, the one named last changes fastest.
Arguments:
- tokens: bfloat16 [64, 512, 768], P(('dp', 'fsdp')), may hold values from -6 to 6
- segments: int32 [64, 512], P(('dp', 'fsdp')), may hold values from 0 to 11, never falling along the last dimension, each value on 1 to 256 neighbouring positions
- w_query: bfloat16 [768, 768], P(('dp', 'fsdp')), may hold values from -0.21875 to 0.21875
- w_key: bfloat16 [768, 768], P(('dp', 'fsdp')), may hold values from -0.21875 to 0.21875
- w_value: bfloat16 [768, 768], P(('dp', 'fsdp')), may hold values from -0.21875 to 0.21875
- w_output: bfloat16 [768, 768], P(('dp', 'fsdp')), may hold values from -1.25 to 1.25
- w_inner: bfloat16 [768, 3072], P(('dp', 'fsdp')), may hold values from -0.21875 to 0.21875
- w_outer: bfloat16 [3072, 768], P(('dp', 'fsdp')), may hold values from -0.109375 to 0.109375
- down_query: bfloat16 [768, 8], P(('dp', 'fsdp')), may hold values from -0.21875 to 0.21875
- down_value: bfloat16 [768, 8], P(('dp', 'fsdp')), may hold values from -0.21875 to 0.21875
- up_query: bfloat16 [8, 768], replicated, may hold values from -0.59765625 to 0.59765625
- up_value: bfloat16 [8, 768], replicated, may hold values from -0.59765625 to 0.59765625
- norm1_gain: float32 [768], replicated, may hold values from 0.5 to 1.5
- norm1_shift: float32 [768], replicated, may hold values from -1.5 to 1.5
- norm2_gain: float32 [768], replicated, may hold values from 0.5 to 1.5
- norm2_shift: float32 [768], replicated, may hold values from -1.5 to 1.5
- out_grad: bfloat16 [64, 512, 768], P(('dp', 'fsdp')), may hold values from -6 to 6
Outputs:
- layer_out: bfloat16 [64, 512, 768], P(('dp', 'fsdp'))
- tokens_grad: bfloat16 [64, 512, 768], P(('dp', 'fsdp'))
- up_query_grad: float32 [8, 768], replicated
- up_value_grad: float32 [8, 768], replicated
Inputs may be any that keep to these rules, and one draw needn't show every extreme that they name: `segments`: within each packed row the segment numbers never fall; each item spans 1 to 256 positions, and some item spans exactly 256.
All inputs are finite; a program needn't handle non-finite values.
Results may differ from a plain program's by a relative error of at most 0.014.
The roundings to bfloat16 on the way count: a program that leaves them out, or rounds other values in their place, can miss the bound.
Values may be sent and summed in bfloat16 or wider, within the bound.
A program may use at most 128 MiB of HBM per device.

v0:
```python
import functools

import jax
import jax.numpy as jnp
from jax import lax
from jax.experimental import pallas as pl
from jax.experimental.pallas import tpu as pltpu
from jax.sharding import PartitionSpec as P

MESH = pl.DeviceIdType.MESH
D, H, HD, FF, R, SEQ = 768, 12, 64, 3072, 8, 512
HALF, PAIRS, LANES = SEQ // 2, H // 2, 128
WIDE = D + LANES
BF, F32 = jnp.bfloat16, jnp.float32
AXES = ("dp", "fsdp")


def dot(a, b):
    return lax.dot_general(a, b, (((1,), (0,)), ((), ())), preferred_element_type=F32)


def dot_nt(a, b):
    return lax.dot_general(a, b, (((1,), (1,)), ((), ())), preferred_element_type=F32)


def dot_tn(a, b):
    return lax.dot_general(a, b, (((0,), (0,)), ((), ())), preferred_element_type=F32)


def mean(v):
    return jnp.mean(v, axis=-1, keepdims=True)


def gelu_parts(u):
    dens = jnp.exp(u * u * -0.5)
    t = 1.0 / (jnp.abs(u) * (0.3275911 * 0.7071067811865476) + 1.0)
    poly = ((((1.061405429 * t - 1.453152027) * t + 1.421413741) * t - 0.284496736) * t + 0.254829592) * t
    tail = poly * dens * 0.5
    phi = jnp.where(u < 0, tail, 1.0 - tail)
    return u * phi, phi + u * dens * 0.3989422804014327


def two_heads(v):
    first = lax.broadcasted_iota(jnp.int32, v.shape, 1) < HD
    zero = jnp.zeros_like(v)
    return jnp.concatenate([jnp.where(first, v, zero), jnp.where(first, zero, v)], axis=0)


def one_pair(v):
    first = lax.broadcasted_iota(jnp.int32, (HALF, 2 * HD), 1) < HD
    return jnp.where(first, v[:HALF], v[HALF:])


def staged(count, *stages):
    held = [None] * count
    for t in range(count + len(stages) - 1):
        for k, stage in enumerate(stages):
            if 0 <= t - k < count:
                held[t - k] = stage(t - k, held[t - k])


class Links:
    def __init__(self, groups, flat, ssem, rsem, lsem):
        self.groups, self.flat, self.ssem, self.rsem, self.lsem = groups, flat, ssem, rsem, lsem
        dp, fs = lax.axis_index("dp"), lax.axis_index("fsdp")
        z, x, y, c = self.z, self.x, self.y, self.c = dp // 2, dp % 2, fs // 2, fs % 2
        xa, ya = jnp.where(c == 0, x, 1 - x), jnp.where(c == 0, 1 - y, y)
        xb, yb = jnp.where(c == 0, 1 - x, x), jnp.where(c == 0, y, 1 - y)
        self.near, self.far = self.device(z, xa, ya, c), self.device(z, xb, yb, c)
        self.twin, self.diag = self.device(z, x, y, 1 - c), self.device(z, 1 - x, 1 - y, c)
        self.line = [self.device((z + d) % 4, x, y, c) for d in (1, 2, 3)]
        self.up, self.down = self.device(jnp.minimum(z + 1, 3), x, y, c), self.device(jnp.maximum(z - 1, 0), x, y, c)
        self.mine, self.at_near, self.at_far, self.at_diag = x * 2 + y, xa * 2 + ya, xb * 2 + yb, 3 - x * 2 - y

    @staticmethod
    def device(z, x, y, c):
        return (z * 2 + x, y * 2 + c)

    def meet(self):
        barrier = pltpu.get_barrier_semaphore()
        others = [to for _, to in self.in_plane()] + self.on_line()[1:]
        for other in others:
            pl.semaphore_signal(barrier, 1, device_id=other, device_id_type=MESH)
        pl.semaphore_wait(barrier, len(others))

    def in_plane(self):
        there = [(n // 4, n // 2 % 2, n % 2) for n in range(1, 8)]
        place = [((self.x + i) % 2, (self.y + j) % 2, (self.c + k) % 2) for i, j, k in there]
        return [(c, self.device(self.z, x, y, c)) for x, y, c in place]

    def on_line(self):
        there = [(0, 1)] + [(d, k) for d in (1, 2, 3) for k in (0, 1)]
        return [self.device((self.z + d) % 4, self.x, self.y, (self.c + k) % 2) for d, k in there]

    def at_column(self, g, chip):
        _, buf, cols = self.groups[g]
        return buf.at[:, chip, self.c, :, :, cols]

    def at_plane(self, g, z):
        _, buf, cols = self.groups[g]
        return buf.at[z, :, self.c, :, :, cols]

    def at_piece(self, g, chip):
        _, buf, cols = self.groups[g]
        return buf.at[self.z, chip, self.c, :, :, cols]

    def send(self, g, src, dst, k, to):
        pltpu.make_async_remote_copy(
            src_ref=src,
            dst_ref=dst,
            send_sem=self.ssem.at[g],
            recv_sem=self.rsem.at[g, k],
            device_id=to,
            device_id_type=MESH,
        ).start()

    @staticmethod
    def wait(ref, sem):
        pltpu.make_async_copy(ref, ref, sem).wait()


    def own(self, g):
        src = self.groups[g][0]
        pltpu.make_async_copy(src, self.at_piece(g, self.mine), self.lsem.at[g]).start()
        for d in range(3):
            self.send(g, src, self.at_piece(g, self.mine), d, self.line[d])

    def column_on(self, g, chip, *to):
        for k, other in to:
            self.send(g, self.at_column(g, chip), self.at_column(g, chip), k, other)

    def after_line(self, g):
        src = self.groups[g][0]
        self.wait(src, self.lsem.at[g])
        for d in range(3):
            self.wait(src, self.rsem.at[g, d])
        self.column_on(g, self.mine, (3, self.near), (4, self.far), (6, self.twin))

    def after_near(self, g):
        self.wait(self.at_column(g, self.at_near), self.rsem.at[g, 3])
        self.column_on(g, self.at_near, (5, self.far), (7, self.twin))

    def after_far(self, g):
        self.wait(self.at_column(g, self.at_far), self.rsem.at[g, 4])
        self.column_on(g, self.at_far, (8, self.twin))

    def after_diag(self, g):
        self.wait(self.at_column(g, self.at_diag), self.rsem.at[g, 5])
        self.column_on(g, self.at_diag, (9, self.twin))

    def whole(self, g):
        for k in range(4):
            self.wait(self.at_column(g, self.mine), self.rsem.at[g, 6 + k])


    def own_flat(self, g):
        src = self.groups[g][0]
        pltpu.make_async_copy(src, self.at_piece(g, self.mine), self.lsem.at[g]).start()
        self.send(g, src, self.at_piece(g, self.mine), 0, self.near)
        self.send(g, src, self.at_piece(g, self.mine), 1, self.far)

    def near_flat(self, g):
        piece = self.at_piece(g, self.at_near)
        self.wait(piece, self.rsem.at[g, 0])
        self.send(g, piece, piece, 2, self.far)

    def plane_on(self, g, z, up, down):
        plane = self.at_plane(g, z)
        if up:
            pl.when(self.z < 3)(lambda: self.send(g, plane, plane, 3 + z, self.up))
        if down:
            pl.when(self.z > 0)(lambda: self.send(g, plane, plane, 3 + z, self.down))
        self.send(g, plane, plane, 7 + z, self.twin)

    def plane_flat(self, g):
        src = self.groups[g][0]
        self.wait(src, self.lsem.at[g])
        self.wait(src, self.rsem.at[g, 1])
        self.wait(src, self.rsem.at[g, 2])
        self.plane_on(g, self.z, True, True)

    def hop_flat(self, d, g):
        def below():
            self.wait(self.at_plane(g, self.z - d), self.rsem.at[g, 3 + self.z - d])
            self.plane_on(g, self.z - d, True, False)

        def above():
            self.wait(self.at_plane(g, self.z + d), self.rsem.at[g, 3 + self.z + d])
            self.plane_on(g, self.z + d, False, True)

        pl.when(self.z >= d)(below)
        pl.when(self.z + d <= 3)(above)

    def whole_flat(self, g):
        for z in range(4):
            self.wait(self.at_plane(g, z), self.rsem.at[g, 7 + z])

    def plan(self):
        first = [g for g in range(len(self.groups)) if g not in self.flat]
        steps = [(self.own, g) for g in first] + [(self.own_flat, g) for g in self.flat]
        stages = (self.after_line, self.after_near, self.after_far, self.after_diag, self.whole)
        main = []
        for t in range(len(first) + len(stages) - 1):
            for k, stage in enumerate(stages):
                if 0 <= t - k < len(first):
                    main.append((stage, first[t - k]))
        side = [self.near_flat, self.plane_flat] + [functools.partial(self.hop_flat, d) for d in (1, 2, 3)]
        when = ((0.12, 0.14), (0.25, 0.30), (0.45, 0.55), (0.65, 0.75), (0.85, 0.95))
        extra = [(f, (stage, g)) for stage, fs in zip(side, when) for f, g in zip(fs, self.flat)]
        for f, item in sorted(extra, key=lambda e: -e[0]):
            main.insert(int(f * len(main)), item)
        return steps, main + [(self.whole_flat, g) for g in self.flat]

    def run(self, works):
        steps, main = self.plan()
        for step, g in steps:
            step(g)
        ends = (self.whole, self.whole_flat)
        here, todo = set(), list(works)
        for step, g in main:
            if todo and todo[0][0] <= here:
                todo.pop(0)[1]()
            step(g)
            if step in ends:
                here.add(g)
        for _, fn in todo:
            fn()

    def drain(self):
        for g, (src, _, _) in enumerate(self.groups):
            for _ in range(3):
                self.wait(src, self.ssem.at[g])
            if g in self.flat:
                plane = self.at_plane(g, 0)
                sent = 4 + jnp.where(self.z < 3, self.z + 1, 0) + jnp.where(self.z > 0, 4 - self.z, 0)
                lax.fori_loop(0, sent, lambda _, v: (self.wait(plane, self.ssem.at[g]), v)[1], 0)
            else:
                for _ in range(7):
                    self.wait(self.at_column(g, self.mine), self.ssem.at[g])


class Local:
    def __init__(self, groups, lsem):
        self.copies = [
            pltpu.make_async_copy(src, buf.at[:, :, :, :, :, cols], lsem.at[g]) for g, (src, buf, cols) in enumerate(groups)
        ]

    def run(self, works):
        for copy in self.copies:
            copy.start()
        here = set()
        for needs, fn in works:
            for g in sorted(needs - here):
                self.copies[g].wait()
            here |= needs
            fn()

    def drain(self):
        pass


class Sums:
    def __init__(self, links, q, v, mine, plane, line, ssem, rsem):
        self.k, self.q, self.v, self.mine, self.plane, self.line = links, q, v, mine, plane, line
        self.ssem, self.rsem, self.sends = ssem, rsem, []

    def copy(self, ref, to_ref, k, to):
        send = pltpu.make_async_remote_copy(
            src_ref=ref,
            dst_ref=to_ref,
            send_sem=self.ssem.at[k],
            recv_sem=self.rsem.at[k],
            device_id=to,
            device_id_type=MESH,
        )
        send.start()
        self.sends.append(send)

    def over_plane(self):
        k = self.k
        slot = self.plane.at[(k.x * 2 + k.y) * 2 + k.c]
        self.mine[0], self.mine[1] = self.q[...], self.v[...]
        self.plane[(k.x * 2 + k.y) * 2 + k.c] = self.mine[k.c]
        for n, (core, to) in enumerate(k.in_plane()):
            self.copy(self.mine.at[core], slot, n, to)

    def end(self):
        for s in self.sends:
            s.wait()
        self.sends = []

    def over_line(self):
        self.end()
        k, p = self.k, self.plane
        self.line[k.c, k.z] = ((p[0] + p[1]) + (p[2] + p[3])) + ((p[4] + p[5]) + (p[6] + p[7]))
        places = self.line.at[k.c, k.z]
        for n, to in enumerate(k.on_line()):
            self.copy(places, places, 7 + n, to)

    def finish(self):
        p = self.line
        for n in range(7):
            pltpu.make_async_copy(p.at[0, 0], p.at[0, 0], self.rsem.at[7 + n]).wait()
            pltpu.make_async_copy(p.at[0, 0], p.at[0, 0], self.ssem.at[7 + n]).wait()
        self.q[...] = (p[0, 0] + p[0, 1]) + (p[0, 2] + p[0, 3])
        self.v[...] = (p[1, 0] + p[1, 1]) + (p[1, 2] + p[1, 3])


def find_turn(seg):
    lane = lax.broadcasted_iota(jnp.int32, (8, SEQ), 1)
    hit = (seg == pltpu.roll(seg, SEQ - HALF + 1, 1)) & (lane <= HALF)
    return jnp.min(jnp.where(hit, lane, SEQ), axis=1, keepdims=True)[0:1]


def turning(by):
    i = lax.broadcasted_iota(jnp.int32, (SEQ, SEQ), 0)
    diff = lax.broadcasted_iota(jnp.int32, (SEQ, SEQ), 1) - i - by
    return jnp.where((diff == 0) | (diff == SEQ) | (diff == -SEQ), 1.0, 0.0).astype(BF)


def layer_kernel(
    remote,
    seg_ref, up_q, up_v, g1, b1, g2, b2, dqt, dvt, x_hbm, g_hbm, wq_h, wk_h, wv_h, wo_h, win_h, wout_h,
    y_hbm, tg_hbm, gq_ref, gv_ref,
    wq_s, wk_s, wv_s, wo_s, win_s, wout_s, own_s, flip_s, up_s,
    x_s, g_s, perm_s, bias_s, low_s, qkv_s, p_s, ctx_s, n1_s, r1_s, hb_s, act_s, gp_s, dz_s, db_s, out_s, two_s,
    ssem, rsem, lsem, iosem, mine_s, plane_s, line_s, ssem2, rsem2,
):
    rows = x_s.shape[0]
    loads = [pltpu.make_async_copy(src, dst, iosem.at[k]) for k, (src, dst) in enumerate(((x_hbm, x_s), (g_hbm, g_s)))]
    for load in loads:
        load.start()

    every, col = slice(None), pl.ds
    groups = [(own_s if remote else wq_h, wq_s, every), (wk_h, wk_s, every), (wv_h, wv_s, every), (wo_h, wo_s, every)]
    lead = (every,) * (2 if remote else 5)
    groups += [(win_h.at[(*lead, col(D * j, D))], win_s, col(D * j, D)) for j in range(4)]
    groups += [(wout_h.at[(*lead, col(HALF * j, HALF))], wout_s, col(HALF * j, HALF)) for j in range(3)]
    wq_g, wk_g, wv_g, wo_g, win_g, wout_g = 0, 1, 2, 3, 4, 8

    if remote:
        stage = pltpu.make_async_copy(wq_h, own_s.at[:, :, col(0, D)], iosem.at[2])
        stage.start()
        flip_s[...] = jnp.zeros_like(flip_s)
        flip_s[0:R, 0 : dqt.shape[1]] = dqt[...].astype(F32)
        flip_s[R : 2 * R, 0 : dvt.shape[1]] = dvt[...].astype(F32)
        downs = flip_s[...].T[0 : dqt.shape[1]].astype(BF)
        own_s[:, :, D:] = downs.reshape(*own_s.shape[:2], LANES)
        net = Links(groups, (wout_g + 1, wout_g + 2), ssem, rsem, lsem)
        net.meet()
        stage.wait()
    else:
        net = Local(groups, lsem)
    zeros = jnp.zeros((R, D), F32)
    up_s[0] = jnp.concatenate([2.0 * up_q[...].astype(F32), zeros], axis=0).astype(BF)
    up_s[1] = jnp.concatenate([zeros, 2.0 * up_v[...].astype(F32)], axis=0).astype(BF)
    gq_ref[...] = jnp.zeros_like(gq_ref)
    gv_ref[...] = jnp.zeros_like(gv_ref)

    def flat(ref, cols=every):
        v = ref[:, :, :, :, :, cols]
        return v.reshape(-1, v.shape[-1])

    def thirds(fn):
        for n in range(3):
            fn(slice(HALF * n, HALF * (n + 1)))

    def each_row(fn, *args):
        def one(r, carry):
            fn(r, *args)
            return carry

        return lambda: lax.fori_loop(0, rows, one, 0)

    def turn(r):
        seg = jnp.broadcast_to(seg_ref[pl.ds(r, 1), :], (8, SEQ))
        perm_s[...] = turning(find_turn(seg))
        segb = seg.astype(F32).astype(BF)
        seg_row = dot_nt(perm_s[HALF:, :], segb)[:, 0:1]
        seg_col = dot_nt(segb, perm_s[HALF:, :])[0:1]
        bias = jnp.where(seg_col == seg_row, 0.0, -1e30)
        bias_s[r, :HALF] = bias
        bias_s[r, HALF:] = bias

        def part(c):
            x_s[r, :, c] = dot(perm_s[...], x_s[r, :, c]).astype(BF)
            g_s[r, :, c] = dot(perm_s[...], g_s[r, :, c]).astype(BF)

        thirds(part)

    def first_turn():
        for load in loads:
            load.wait()
        each_row(turn)()

    def project(r):
        low_s[r] = dot(x_s[r], flat(wq_s, slice(D, D + 2 * R))).astype(BF)

        def part(c):
            qkv_s[r, :, c] = (dot(x_s[r], flat(wq_s, c)) + dot(low_s[r], up_s[0, :, c])).astype(BF)

        thirds(part)

    def project_k(r):
        def part(c):
            qkv_s[r, :, D + c.start : D + c.stop] = dot(x_s[r], flat(wk_s, c)).astype(BF)

        thirds(part)

    def project_v(r):
        def part(c):
            v = dot(x_s[r], flat(wv_s, c)) + dot(low_s[r], up_s[1, :, c])
            qkv_s[r, :, 2 * D + c.start : 2 * D + c.stop] = v.astype(BF)

        thirds(part)

    def item(i, n):
        p, b = 2 * i + n // 2, n % 2
        return p, b, slice(HALF * b, HALF * (b + 1)), [pl.ds(pl.multiple_of(D * w + LANES * p, LANES), LANES) for w in range(3)]

    def heads(r):
        def some(i, carry):
            def scores(n, _):
                p, b, span, cut = item(i, n)
                s = dot_nt(two_heads(qkv_s[r, span, cut[0]] * 0.125), qkv_s[r, span, cut[1]])
                return s + bias_s[r] if b == 1 else s

            def soften(n, s):
                p, b, _, _ = item(i, n)
                e = jnp.exp(s - jnp.max(s, axis=1, keepdims=True))
                probs = (e * (1.0 / jnp.sum(e, axis=1, keepdims=True))).astype(BF)
                p_s[r, p, b] = probs
                return probs

            def context(n, probs):
                p, b, span, cut = item(i, n)
                ctx_s[r, span, cut[0]] = one_pair(dot(probs, qkv_s[r, span, cut[2]])).astype(BF)

            staged(4, scores, soften, context)
            return carry

        lax.fori_loop(0, PAIRS // 2, some, 0)

    def attended(r):
        z1 = x_s[r].astype(F32) + dot(ctx_s[r], flat(wo_s))
        z1 = z1 - mean(z1)
        r1 = lax.rsqrt(mean(z1 * z1) + 1e-5)
        n1 = z1 * r1
        n1_s[r] = n1
        r1_s[r] = r1
        hb_s[r] = (n1 * g1[...][None] + b1[...][None]).astype(BF)

    def inner(r, j):
        for n in range(3):
            c = slice(D * j + HALF * n, D * j + HALF * (n + 1))
            act, slope = gelu_parts(dot(hb_s[r], flat(win_s, c)))
            act_s[r, :, c] = act.astype(BF)
            gp_s[r, :, c] = slope.astype(BF)

    def outer(r, j):
        c = slice(HALF * j, HALF * (j + 1))
        h1 = n1_s[r, :, c] * g1[...][None, c] + b1[...][None, c]
        dz_s[r, :, c] = h1 + dot(act_s[r], flat(wout_s, c))

    def second_norm(r):
        z2 = dz_s[r]
        z2 = z2 - mean(z2)
        r2 = lax.rsqrt(mean(z2 * z2) + 1e-5)
        n2 = z2 * r2
        out_s[r] = (n2 * g2[...][None] + b2[...][None]).astype(BF)
        pltpu.make_async_copy(out_s.at[r], y_hbm.at[r], iosem.at[3]).start()
        dn2 = g_s[r].astype(F32) * g2[...][None]
        dz2 = r2 * (dn2 - mean(dn2) - n2 * mean(dn2 * n2))
        dz_s[r] = dz2
        db_s[...] = dz2.astype(BF)

    def inner_back(r):
        for n in range(4):
            c = slice(D * n, D * (n + 1))
            dact = dot_nt(db_s[...], wout_s[n].reshape(D, D))
            act_s[r, :, c] = (dact * gp_s[r, :, c].astype(F32)).astype(BF)

    def first_norm_back(r):
        dn1 = (dz_s[r] + dot_nt(act_s[r], flat(win_s))) * g1[...][None]
        n1 = n1_s[r]
        dz1 = r1_s[r] * (dn1 - mean(dn1) - n1 * mean(dn1 * n1))
        dz_s[r] = dz1
        ctx_s[r] = dot_nt(dz1.astype(BF), flat(wo_s)).astype(BF)

    def heads_back(t, carry):
        r, i = t // (PAIRS // 2), t % (PAIRS // 2)

        def to(n):
            return slice(HALF * (n % 2), HALF * (n % 2 + 1)), slice(LANES * (n // 2), LANES * (n // 2 + 1))

        def values(n, _):
            p, b, span, cut = item(i, n)
            dc = two_heads(ctx_s[r, span, cut[0]])
            dp = dot_nt(dc, qkv_s[r, span, cut[2]])
            two_s[2, *to(n)] = dot_tn(dc, p_s[r, p, b]).T.astype(BF)
            return dp

        def scores(n, dp):
            p, b, _, _ = item(i, n)
            probs = p_s[r, p, b].astype(F32)
            return (probs * (dp - jnp.sum(probs * dp, axis=1, keepdims=True))).astype(BF)

        def sides(n, ds):
            p, b, span, cut = item(i, n)
            q, k = qkv_s[r, span, cut[0]], qkv_s[r, span, cut[1]]
            two_s[0, *to(n)] = (one_pair(dot(ds, k)) * 0.125).astype(BF)
            two_s[1, *to(n)] = dot_tn(two_heads(q * 0.125), ds).T.astype(BF)

        staged(4, values, scores, sides)
        for w in range(3):
            qkv_s[r, :, pl.ds(pl.multiple_of(D * w + 2 * LANES * i, LANES), 2 * LANES)] = two_s[w]
        return carry

    def grads(r):
        gq_ref[...] += 2.0 * dot_tn(low_s[r], qkv_s[r, :, :D])[:R]
        gv_ref[...] += 2.0 * dot_tn(low_s[r], qkv_s[r, :, 2 * D :])[R:]

    def back(r):
        second_norm(r)
        inner_back(r)
        first_norm_back(r)

    def tokens_back(r):
        dq, dk, dv = (qkv_s[r, :, D * w : D * (w + 1)] for w in range(3))
        dlow = (dot_nt(dq, up_s[0]) + dot_nt(dv, up_s[1])).astype(BF)
        tg = dz_s[r] + dot_nt(dq, flat(wq_s, slice(0, D))) + dot_nt(dk, flat(wk_s)) + dot_nt(dv, flat(wv_s))
        out_s[r] = (tg + dot_nt(dlow, flat(wq_s, slice(D, D + 2 * R)))).astype(BF)
        pltpu.make_async_copy(out_s.at[r], tg_hbm.at[r], iosem.at[4]).start()

    works = [
        (set(), first_turn),
        ({wq_g}, each_row(project)),
        ({wk_g}, each_row(project_k)),
        ({wv_g}, each_row(project_v)),
    ]
    works += [({wv_g}, functools.partial(heads, r)) for r in range(rows)]
    works += [({wo_g}, each_row(attended))]
    works += [({win_g + j}, functools.partial(inner, r, j)) for j in range(4) for r in range(rows)]
    works += [({wout_g + j}, each_row(outer, j)) for j in range(3)]
    net.run(works)
    each_row(back)()
    lax.fori_loop(0, rows * PAIRS // 2, heads_back, 0)
    each_row(grads)()
    pltpu.make_async_copy(out_s, y_hbm, iosem.at[3]).wait()
    if remote:
        sums = Sums(net, gq_ref, gv_ref, mine_s, plane_s, line_s, ssem2, rsem2)
        sums.over_plane()

        def last(r, carry):
            tokens_back(r)
            pl.when(r == 0)(sums.over_line)
            return carry

        lax.fori_loop(0, rows, last, 0)
        net.drain()
        sums.finish()
    else:
        each_row(tokens_back)()
    pltpu.make_async_copy(out_s, tg_hbm, iosem.at[4]).wait()


def unturn_kernel(seg_ref, y_ref, tg_ref, gq_ref, gv_ref, oy_ref, otg_ref, oq_ref, ov_ref, perm_s):
    perm_s[...] = turning(-find_turn(jnp.broadcast_to(seg_ref[pl.ds(pl.program_id(0), 1), :], (8, SEQ))))
    oy_ref[0] = dot(perm_s[...], y_ref[0]).astype(BF)
    otg_ref[0] = dot(perm_s[...], tg_ref[0]).astype(BF)
    oq_ref[...] = gq_ref[...]
    ov_ref[...] = gv_ref[...]


def unturn(seg, y, tg, gq, gv):
    def whole(v):
        return pl.BlockSpec(v.shape, lambda r: (0, 0))

    part = pl.BlockSpec((1, SEQ, D), lambda r: (r, 0, 0))
    act, grad = jax.ShapeDtypeStruct(y.shape, BF), jax.ShapeDtypeStruct(gq.shape, F32)
    return pl.pallas_call(
        unturn_kernel,
        grid=(y.shape[0],),
        out_shape=[act, act, grad, grad],
        in_specs=[whole(seg), part, part, whole(gq), whole(gv)],
        out_specs=[part, part, whole(gq), whole(gv)],
        scratch_shapes=[pltpu.VMEM((SEQ, SEQ), BF)],
        name="unturn",
    )(seg, y, tg, gq, gv)


def run_layer(remote, seg, x, g, mats, downs, ups, norms):
    rows = x.shape[0]
    vmem, hbm = pl.BlockSpec(memory_space=pltpu.VMEM), pl.BlockSpec(memory_space=pl.ANY)
    act, grad = jax.ShapeDtypeStruct(x.shape, BF), jax.ShapeDtypeStruct((R, D), F32)
    blocks = 11
    shapes = [
        ((4, 4, 2, 3, 8, WIDE), BF),
        ((4, 4, 2, 3, 8, D), BF),
        ((4, 4, 2, 3, 8, D), BF),
        ((4, 4, 2, 3, 8, D), BF),
        ((4, 4, 2, 3, 8, FF), BF),
        ((4, 4, 2, 12, 8, D), BF),
        ((3, 8, WIDE), BF),
        ((LANES, LANES), F32),
        ((2, 2 * R, D), BF),
        ((rows, SEQ, D), BF),
        ((rows, SEQ, D), BF),
        ((SEQ, SEQ), BF),
        ((rows, SEQ, HALF), F32),
        ((rows, SEQ, 2 * R), BF),
        ((rows, SEQ, 3 * D), BF),
        ((rows, PAIRS, 2, SEQ, HALF), BF),
        ((rows, SEQ, D), BF),
        ((rows, SEQ, D), F32),
        ((rows, SEQ, 1), F32),
        ((rows, SEQ, D), BF),
        ((rows, SEQ, FF), BF),
        ((rows, SEQ, FF), BF),
        ((rows, SEQ, D), F32),
        ((SEQ, D), BF),
        ((rows, SEQ, D), BF),
        ((3, SEQ, 2 * LANES), BF),
    ]
    dma = pltpu.SemaphoreType.DMA
    return pl.pallas_call(
        functools.partial(layer_kernel, remote),
        out_shape=[act, act, grad, grad],
        in_specs=[vmem] * 9 + [hbm] * 8,
        out_specs=[hbm, hbm, vmem, vmem],
        scratch_shapes=[pltpu.VMEM(*s) for s in shapes]
        + [dma((blocks,)), dma((blocks, 11)), dma((blocks,)), dma((5,))]
        + [pltpu.VMEM((n, R, D), F32) for n in (2, 8)] + [pltpu.VMEM((2, 4, R, D), F32), dma((14,)), dma((14,))],
        compiler_params=pltpu.CompilerParams(
            vmem_limit_bytes=64 << 20,
            **({"collective_id": 0, "has_side_effects": True} if remote else {}),
        ),
        name="layer",
    )(seg, *ups, *norms, *downs, x, g, *mats)


def solution(mesh):
    remote = dict(mesh.shape) == {"dp": 8, "fsdp": 4}

    def body(
        tokens, segments, w_query, w_key, w_value, w_output, w_inner, w_outer, down_query, down_value,
        up_query, up_value, norm1_gain, norm1_shift, norm2_gain, norm2_shift, out_grad,
    ):
        mats = [w_query, w_key, w_value, w_output, w_inner, w_outer]
        if remote:
            mats = [m.reshape(-1, 8, m.shape[1]) for m in mats]
        else:
            pad = jnp.zeros((w_query.shape[0], LANES - 2 * R), BF)
            mats[0] = jnp.concatenate([w_query, down_query, down_value, pad], axis=1)
            mats = [lax.all_gather(m, AXES, axis=0, tiled=True) for m in mats]
            mats = [m.reshape(4, 4, 2, -1, 8, m.shape[1]) for m in mats]
        y, tg, gq, gv = run_layer(
            remote,
            segments,
            tokens,
            out_grad,
            mats,
            (down_query.T, down_value.T),
            (up_query, up_value),
            (norm1_gain, norm1_shift, norm2_gain, norm2_shift),
        )
        if not remote:
            gq, gv = lax.psum((gq, gv), AXES)
        return unturn(segments, y, tg, gq, gv)

    split, copied = P(AXES), P()
    return jax.shard_map(
        body,
        mesh=mesh,
        in_specs=(split,) * 10 + (copied,) * 6 + (split,),
        out_specs=(split, split, copied, copied),
        check_vma=False,
    )
```

profile of v0, /device:TPU:0, one launch (start us, length us, event | category | flops | bytes accessed | tf_op | source)
XLA Modules:
  0.0 120.2 jit_solution(16171051888715556004)
XLA Ops:
  0.6 114.7 %layer.1 = (bf16[2,512,768]{2,1,0:T(8,128)(2,1)}, bf16[2,512,768]{2,1,0:T(8,128)(2,1)}, f32[8,768]{1,0:T(8,128)}, f32[8,768]{1,0:T(8,128)}) custom-call(s32[2,512]{1,0:T(2,128)} %seg_ref.3, bf16[8,768]{1,0:T(8,128)(2,1)} %up_q.1, bf16[8,768]{1,0:T(8,128)(2,1)} %up_v.1, f32[768]{0:T(1024)} %g1.1, f32[768]{0:T(1024)} %b1.1, f32[768]{0:T(1024)} %g2.1, f32[768]{0:T(1024)} %b2.1, ...), custom_call_target="tpu_custom_call" | custom-call | tf_op jit(solution)/shard_map/layer/pallas_call | solution.py:626
  115.4 4.9 %unturn.1 = (bf16[2,512,768]{2,1,0:T(8,128)(2,1)}, bf16[2,512,768]{2,1,0:T(8,128)(2,1)}, f32[8,768]{1,0:T(8,128)}, f32[8,768]{1,0:T(8,128)}) custom-call(s32[2,512]{1,0:T(2,128)} %seg_ref.3, bf16[2,512,768]{2,1,0:T(8,128)(2,1)} %get-tuple-element.8.y_ref, bf16[2,512,768]{2,1,0:T(8,128)(2,1)} %get-tuple-element.9.tg_ref, f32[8,768]{1,0:T(8,128)} %get-tuple-element.10.gq_ref, ...), custom_call_target="tpu_custom_call" | custom-call | tf_op jit(solution)/shard_map/unturn/pallas_call | solution.py:581
where the time goes:
time: 120 us
  Pallas kernels  120 us (100%)
    pallas_call x1, Pallas kernels, run_layer(): pl.pallas_call(functools.partial(layer_kernel, remote), out_shape=[act, a...  115 us
    pallas_call x1, Pallas kernels, unturn(): pl.pallas_call(unturn_kernel, grid=(y.shape[0],), out_shape=[act, act, gr...  4.87 us

commit v1 on v0

--- a/solution.py
+++ b/solution.py
@@ -60,7 +60,8 @@
 
 
 class Links:
-    def __init__(self, groups, flat, ssem, rsem, lsem):
+    def __init__(self, groups, flat, early, ssem, rsem, lsem):
+        self.early = early
         self.groups, self.flat, self.ssem, self.rsem, self.lsem = groups, flat, ssem, rsem, lsem
         dp, fs = lax.axis_index("dp"), lax.axis_index("fsdp")
         z, x, y, c = self.z, self.x, self.y, self.c = dp // 2, dp % 2, fs // 2, fs % 2
@@ -124,6 +125,9 @@
         pltpu.make_async_copy(src, self.at_piece(g, self.mine), self.lsem.at[g]).start()
         for d in range(3):
             self.send(g, src, self.at_piece(g, self.mine), d, self.line[d])
+        if g in self.early:
+            self.send(g, src, self.at_piece(g, self.mine), 3, self.near)
+            self.send(g, src, self.at_piece(g, self.mine), 4, self.far)
 
     def column_on(self, g, chip, *to):
         for k, other in to:
@@ -134,7 +138,15 @@
         self.wait(src, self.lsem.at[g])
         for d in range(3):
             self.wait(src, self.rsem.at[g, d])
-        self.column_on(g, self.mine, (3, self.near), (4, self.far), (6, self.twin))
+        if g in self.early:
+            _, buf, cols = self.groups[g]
+            for k, other in ((3, self.near), (4, self.far)):
+                for d in (1, 2, 3):
+                    piece = buf.at[(self.z + d) % 4, self.mine, self.c, :, :, cols]
+                    self.send(g, piece, piece, k, other)
+            self.column_on(g, self.mine, (6, self.twin))
+        else:
+            self.column_on(g, self.mine, (3, self.near), (4, self.far), (6, self.twin))
 
     def after_near(self, g):
         self.wait(self.at_column(g, self.at_near), self.rsem.at[g, 3])
@@ -226,6 +238,9 @@
         for _, fn in todo:
             fn()
 
+    def need(self, *groups):
+        pass
+
     def drain(self):
         for g, (src, _, _) in enumerate(self.groups):
             for _ in range(3):
@@ -255,6 +270,10 @@
             here |= needs
             fn()
 
+    def need(self, *groups):
+        for g in groups:
+            self.copies[g].wait()
+
     def drain(self):
         pass
 
@@ -323,7 +342,7 @@
     seg_ref, up_q, up_v, g1, b1, g2, b2, dqt, dvt, x_hbm, g_hbm, wq_h, wk_h, wv_h, wo_h, win_h, wout_h,
     y_hbm, tg_hbm, gq_ref, gv_ref,
     wq_s, wk_s, wv_s, wo_s, win_s, wout_s, own_s, flip_s, up_s,
-    x_s, g_s, perm_s, bias_s, low_s, qkv_s, p_s, ctx_s, n1_s, r1_s, hb_s, act_s, gp_s, dz_s, db_s, out_s, two_s,
+    x_s, g_s, perm_s, bias_s, low_s, qkv_s, p_s, ctx_s, n1_s, r1_s, hb_s, act_s, gp_s, dz_s, out_s, two_s,
     ssem, rsem, lsem, iosem, mine_s, plane_s, line_s, ssem2, rsem2,
 ):
     rows = x_s.shape[0]
@@ -346,7 +365,7 @@
         flip_s[R : 2 * R, 0 : dvt.shape[1]] = dvt[...].astype(F32)
         downs = flip_s[...].T[0 : dqt.shape[1]].astype(BF)
         own_s[:, :, D:] = downs.reshape(*own_s.shape[:2], LANES)
-        net = Links(groups, (wout_g + 1, wout_g + 2), ssem, rsem, lsem)
+        net = Links(groups, (wout_g + 1, wout_g + 2), (0, 1, 2, 3, 4), ssem, rsem, lsem)
         net.meet()
         stage.wait()
     else:
@@ -372,6 +391,13 @@
 
         return lambda: lax.fori_loop(0, rows, one, 0)
 
+    def each_half(fn, *args):
+        def one(t, carry):
+            fn(t // 2, pl.ds(pl.multiple_of(HALF * (t % 2), HALF), HALF), *args)
+            return carry
+
+        return lambda: lax.fori_loop(0, 2 * rows, one, 0)
+
     def turn(r):
         seg = jnp.broadcast_to(seg_ref[pl.ds(r, 1), :], (8, SEQ))
         perm_s[...] = turning(find_turn(seg))
@@ -457,35 +483,53 @@
             act_s[r, :, c] = act.astype(BF)
             gp_s[r, :, c] = slope.astype(BF)
 
-    def outer(r, j):
+    def outer(r, span, j):
         c = slice(HALF * j, HALF * (j + 1))
-        h1 = n1_s[r, :, c] * g1[...][None, c] + b1[...][None, c]
-        dz_s[r, :, c] = h1 + dot(act_s[r], flat(wout_s, c))
-
-    def second_norm(r):
-        z2 = dz_s[r]
-        z2 = z2 - mean(z2)
-        r2 = lax.rsqrt(mean(z2 * z2) + 1e-5)
-        n2 = z2 * r2
-        out_s[r] = (n2 * g2[...][None] + b2[...][None]).astype(BF)
-        pltpu.make_async_copy(out_s.at[r], y_hbm.at[r], iosem.at[3]).start()
-        dn2 = g_s[r].astype(F32) * g2[...][None]
-        dz2 = r2 * (dn2 - mean(dn2) - n2 * mean(dn2 * n2))
-        dz_s[r] = dz2
-        db_s[...] = dz2.astype(BF)
-
-    def inner_back(r):
-        for n in range(4):
-            c = slice(D * n, D * (n + 1))
-            dact = dot_nt(db_s[...], wout_s[n].reshape(D, D))
-            act_s[r, :, c] = (dact * gp_s[r, :, c].astype(F32)).astype(BF)
-
-    def first_norm_back(r):
-        dn1 = (dz_s[r] + dot_nt(act_s[r], flat(win_s))) * g1[...][None]
-        n1 = n1_s[r]
-        dz1 = r1_s[r] * (dn1 - mean(dn1) - n1 * mean(dn1 * n1))
-        dz_s[r] = dz1
-        ctx_s[r] = dot_nt(dz1.astype(BF), flat(wo_s)).astype(BF)
+        return n1_s[r, span, c] * g1[...][None, c] + b1[...][None, c] + dot(act_s[r, span], flat(wout_s, c))
+
+    def outer_first(r):
+        dz_s[r, :, 0:HALF] = outer(r, slice(None), 0)
+
+    def back(r):
+        spans = [slice(HALF * b, HALF * (b + 1)) for b in range(2)]
+
+        def summed(b, _):
+            return [outer(r, spans[b], j) for j in (1, 2)]
+
+        def second_norm(b, last):
+            span = spans[b]
+            z2 = jnp.concatenate([dz_s[r, span, 0:HALF], *last], axis=1)
+            z2 = z2 - mean(z2)
+            r2 = lax.rsqrt(mean(z2 * z2) + 1e-5)
+            n2 = z2 * r2
+            out_s[r, span] = (n2 * g2[...][None] + b2[...][None]).astype(BF)
+            pltpu.make_async_copy(out_s.at[r, span], y_hbm.at[r, span], iosem.at[3]).start()
+            dn2 = g_s[r, span].astype(F32) * g2[...][None]
+            dz2 = r2 * (dn2 - mean(dn2) - n2 * mean(dn2 * n2))
+            dz_s[r, span] = dz2
+            return dz2.astype(BF)
+
+        def inner_back(b, df):
+            for n in range(4):
+                c = slice(D * n, D * (n + 1))
+                dact = dot_nt(df, wout_s[n].reshape(D, D))
+                act_s[r, spans[b], c] = (dact * gp_s[r, spans[b], c].astype(F32)).astype(BF)
+
+        def hidden_back(b, _):
+            return dot_nt(act_s[r, spans[b]], flat(win_s))
+
+        def first_norm(b, dh):
+            span = spans[b]
+            dn1 = (dz_s[r, span] + dh) * g1[...][None]
+            n1 = n1_s[r, span]
+            dz1 = r1_s[r, span] * (dn1 - mean(dn1) - n1 * mean(dn1 * n1))
+            dz_s[r, span] = dz1
+            return dz1.astype(BF)
+
+        def context_back(b, dz1):
+            ctx_s[r, spans[b]] = dot_nt(dz1, flat(wo_s)).astype(BF)
+
+        staged(2, summed, second_norm, inner_back, hidden_back, first_norm, context_back)
 
     def heads_back(t, carry):
         r, i = t // (PAIRS // 2), t % (PAIRS // 2)
@@ -520,17 +564,12 @@
         gq_ref[...] += 2.0 * dot_tn(low_s[r], qkv_s[r, :, :D])[:R]
         gv_ref[...] += 2.0 * dot_tn(low_s[r], qkv_s[r, :, 2 * D :])[R:]
 
-    def back(r):
-        second_norm(r)
-        inner_back(r)
-        first_norm_back(r)
-
-    def tokens_back(r):
-        dq, dk, dv = (qkv_s[r, :, D * w : D * (w + 1)] for w in range(3))
+    def tokens_back(r, span):
+        dq, dk, dv = (qkv_s[r, span, D * w : D * (w + 1)] for w in range(3))
         dlow = (dot_nt(dq, up_s[0]) + dot_nt(dv, up_s[1])).astype(BF)
-        tg = dz_s[r] + dot_nt(dq, flat(wq_s, slice(0, D))) + dot_nt(dk, flat(wk_s)) + dot_nt(dv, flat(wv_s))
-        out_s[r] = (tg + dot_nt(dlow, flat(wq_s, slice(D, D + 2 * R)))).astype(BF)
-        pltpu.make_async_copy(out_s.at[r], tg_hbm.at[r], iosem.at[4]).start()
+        tg = dz_s[r, span] + dot_nt(dq, flat(wq_s, slice(0, D))) + dot_nt(dk, flat(wk_s)) + dot_nt(dv, flat(wv_s))
+        out_s[r, span] = (tg + dot_nt(dlow, flat(wq_s, slice(D, D + 2 * R)))).astype(BF)
+        pltpu.make_async_copy(out_s.at[r, span], tg_hbm.at[r, span], iosem.at[4]).start()
 
     works = [
         (set(), first_turn),
@@ -541,8 +580,9 @@
     works += [({wv_g}, functools.partial(heads, r)) for r in range(rows)]
     works += [({wo_g}, each_row(attended))]
     works += [({win_g + j}, functools.partial(inner, r, j)) for j in range(4) for r in range(rows)]
-    works += [({wout_g + j}, each_row(outer, j)) for j in range(3)]
+    works += [({wout_g}, each_row(outer_first))]
     net.run(works)
+    net.need(wout_g + 1, wout_g + 2)
     each_row(back)()
     lax.fori_loop(0, rows * PAIRS // 2, heads_back, 0)
     each_row(grads)()
@@ -551,16 +591,15 @@
         sums = Sums(net, gq_ref, gv_ref, mine_s, plane_s, line_s, ssem2, rsem2)
         sums.over_plane()
 
-        def last(r, carry):
-            tokens_back(r)
-            pl.when(r == 0)(sums.over_line)
-            return carry
-
-        lax.fori_loop(0, rows, last, 0)
+        def last(r, span):
+            tokens_back(r, span)
+            pl.when((r == 0) & (span.start > 0))(sums.over_line)
+
+        each_half(last)()
         net.drain()
         sums.finish()
     else:
-        each_row(tokens_back)()
+        each_half(tokens_back)()
     pltpu.make_async_copy(out_s, tg_hbm, iosem.at[4]).wait()
 
 
@@ -618,7 +657,6 @@
         ((rows, SEQ, FF), BF),
         ((rows, SEQ, FF), BF),
         ((rows, SEQ, D), F32),
-        ((SEQ, D), BF),
         ((rows, SEQ, D), BF),
         ((3, SEQ, 2 * LANES), BF),
     ]

time: 120 us -> 117 us (0.975)
  Pallas kernels: 120 us -> 116 us
    pallas_call x1, Pallas kernels: 115 us -> 111 us  [run_layer(): pl.pallas_call(functools.partial(layer_kernel, remote), out_shape=[act, a...]
where the time goes in v1:
time: 117 us
  Pallas kernels  116 us (99%)
    pallas_call x1, Pallas kernels, run_layer(): pl.pallas_call(functools.partial(layer_kernel, remote), out_shape=[act, a...  111 us
    pallas_call x1, Pallas kernels, unturn(): pl.pallas_call(unturn_kernel, grid=(y.shape[0],), out_shape=[act, act, gr...  4.85 us

profile of v1, /device:TPU:0, one launch (start us, length us, event | category | flops | bytes accessed | tf_op | source)
XLA Modules:
  0.0 116.8 jit_solution(6090820431019382877)
XLA Ops:
  0.6 111.3 %layer.1 = (bf16[2,512,768]{2,1,0:T(8,128)(2,1)}, bf16[2,512,768]{2,1,0:T(8,128)(2,1)}, f32[8,768]{1,0:T(8,128)}, f32[8,768]{1,0:T(8,128)}) custom-call(s32[2,512]{1,0:T(2,128)} %seg_ref.3, bf16[8,768]{1,0:T(8,128)(2,1)} %up_q.1, bf16[8,768]{1,0:T(8,128)(2,1)} %up_v.1, f32[768]{0:T(1024)} %g1.1, f32[768]{0:T(1024)} %b1.1, f32[768]{0:T(1024)} %g2.1, f32[768]{0:T(1024)} %b2.1, ...), custom_call_target="tpu_custom_call" | custom-call | tf_op jit(solution)/shard_map/layer/pallas_call | solution.py:664
  111.9 4.9 %unturn.1 = (bf16[2,512,768]{2,1,0:T(8,128)(2,1)}, bf16[2,512,768]{2,1,0:T(8,128)(2,1)}, f32[8,768]{1,0:T(8,128)}, f32[8,768]{1,0:T(8,128)}) custom-call(s32[2,512]{1,0:T(2,128)} %seg_ref.3, bf16[2,512,768]{2,1,0:T(8,128)(2,1)} %get-tuple-element.8.y_ref, bf16[2,512,768]{2,1,0:T(8,128)(2,1)} %get-tuple-element.9.tg_ref, f32[8,768]{1,0:T(8,128)} %get-tuple-element.10.gq_ref, ...), custom_call_target="tpu_custom_call" | custom-call | tf_op jit(solution)/shard_map/unturn/pallas_call | solution.py:620

commit v2 on v1

--- a/solution.py
+++ b/solution.py
@@ -32,10 +32,10 @@
 
 
 def gelu_parts(u):
-    dens = jnp.exp(u * u * -0.5)
+    dens = jnp.exp2(u * u * -0.7213475204444817)
     t = 1.0 / (jnp.abs(u) * (0.3275911 * 0.7071067811865476) + 1.0)
-    poly = ((((1.061405429 * t - 1.453152027) * t + 1.421413741) * t - 0.284496736) * t + 0.254829592) * t
-    tail = poly * dens * 0.5
+    poly = (((0.5307027145 * t - 0.7265760135) * t + 0.7107068705) * t - 0.142248368) * t + 0.127414796
+    tail = poly * t * dens
     phi = jnp.where(u < 0, tail, 1.0 - tail)
     return u * phi, phi + u * dens * 0.3989422804014327
 
@@ -551,21 +551,29 @@
 
         def sides(n, ds):
             p, b, span, cut = item(i, n)
-            q, k = qkv_s[r, span, cut[0]], qkv_s[r, span, cut[1]]
-            two_s[0, *to(n)] = (one_pair(dot(ds, k)) * 0.125).astype(BF)
-            two_s[1, *to(n)] = dot_tn(two_heads(q * 0.125), ds).T.astype(BF)
+            two_s[0, *to(n)] = (one_pair(dot(ds, qkv_s[r, span, cut[1]])) * 0.125).astype(BF)
+            p_s[r, p, b] = ds
 
         staged(4, values, scores, sides)
-        for w in range(3):
-            qkv_s[r, :, pl.ds(pl.multiple_of(D * w + 2 * LANES * i, LANES), 2 * LANES)] = two_s[w]
+        hb_s[r, :, pl.ds(pl.multiple_of(2 * LANES * i, LANES), 2 * LANES)] = two_s[0]
+        qkv_s[r, :, pl.ds(pl.multiple_of(2 * D + 2 * LANES * i, LANES), 2 * LANES)] = two_s[2]
         return carry
 
+    def keys_back(t, carry):
+        r, i = t // (PAIRS // 2), t % (PAIRS // 2)
+        for n in range(4):
+            p, b, span, cut = item(i, n)
+            dk = dot_tn(two_heads(qkv_s[r, span, cut[0]] * 0.125), p_s[r, p, b]).T.astype(BF)
+            two_s[1, span, LANES * (n // 2) : LANES * (n // 2 + 1)] = dk
+        qkv_s[r, :, pl.ds(pl.multiple_of(D + 2 * LANES * i, LANES), 2 * LANES)] = two_s[1]
+        return carry
+
     def grads(r):
-        gq_ref[...] += 2.0 * dot_tn(low_s[r], qkv_s[r, :, :D])[:R]
+        gq_ref[...] += 2.0 * dot_tn(low_s[r], hb_s[r])[:R]
         gv_ref[...] += 2.0 * dot_tn(low_s[r], qkv_s[r, :, 2 * D :])[R:]
 
     def tokens_back(r, span):
-        dq, dk, dv = (qkv_s[r, span, D * w : D * (w + 1)] for w in range(3))
+        dq, dk, dv = hb_s[r, span], qkv_s[r, span, D : 2 * D], qkv_s[r, span, 2 * D :]
         dlow = (dot_nt(dq, up_s[0]) + dot_nt(dv, up_s[1])).astype(BF)
         tg = dz_s[r, span] + dot_nt(dq, flat(wq_s, slice(0, D))) + dot_nt(dk, flat(wk_s)) + dot_nt(dv, flat(wv_s))
         out_s[r, span] = (tg + dot_nt(dlow, flat(wq_s, slice(D, D + 2 * R)))).astype(BF)
@@ -590,15 +598,13 @@
     if remote:
         sums = Sums(net, gq_ref, gv_ref, mine_s, plane_s, line_s, ssem2, rsem2)
         sums.over_plane()
-
-        def last(r, span):
-            tokens_back(r, span)
-            pl.when((r == 0) & (span.start > 0))(sums.over_line)
-
-        each_half(last)()
+        lax.fori_loop(0, rows * PAIRS // 2, keys_back, 0)
+        sums.over_line()
+        each_half(tokens_back)()
         net.drain()
         sums.finish()
     else:
+        lax.fori_loop(0, rows * PAIRS // 2, keys_back, 0)
         each_half(tokens_back)()
     pltpu.make_async_copy(out_s, tg_hbm, iosem.at[4]).wait()
 

time: 117 us -> 115 us (0.983)
  Pallas kernels: 116 us -> 114 us
    pallas_call x1, Pallas kernels: 111 us -> 109 us  [run_layer(): pl.pallas_call(functools.partial(layer_kernel, remote), out_shape=[act, a...]
where the time goes in v2:
time: 115 us
  Pallas kernels  114 us (99%)
    pallas_call x1, Pallas kernels, run_layer(): pl.pallas_call(functools.partial(layer_kernel, remote), out_shape=[act, a...  109 us
    pallas_call x1, Pallas kernels, unturn(): pl.pallas_call(unturn_kernel, grid=(y.shape[0],), out_shape=[act, act, gr...  4.85 us

profile of v2, /device:TPU:0, one launch (start us, length us, event | category | flops | bytes accessed | tf_op | source)
XLA Modules:
  0.0 114.8 jit_solution(4128846617581325251)
XLA Ops:
  0.6 109.3 %layer.1 = (bf16[2,512,768]{2,1,0:T(8,128)(2,1)}, bf16[2,512,768]{2,1,0:T(8,128)(2,1)}, f32[8,768]{1,0:T(8,128)}, f32[8,768]{1,0:T(8,128)}) custom-call(s32[2,512]{1,0:T(2,128)} %seg_ref.3, bf16[8,768]{1,0:T(8,128)(2,1)} %up_q.1, bf16[8,768]{1,0:T(8,128)(2,1)} %up_v.1, f32[768]{0:T(1024)} %g1.1, f32[768]{0:T(1024)} %b1.1, f32[768]{0:T(1024)} %g2.1, f32[768]{0:T(1024)} %b2.1, ...), custom_call_target="tpu_custom_call" | custom-call | tf_op jit(solution)/shard_map/layer/pallas_call | solution.py:670
  110.0 4.9 %unturn.1 = (bf16[2,512,768]{2,1,0:T(8,128)(2,1)}, bf16[2,512,768]{2,1,0:T(8,128)(2,1)}, f32[8,768]{1,0:T(8,128)}, f32[8,768]{1,0:T(8,128)}) custom-call(s32[2,512]{1,0:T(2,128)} %seg_ref.3, bf16[2,512,768]{2,1,0:T(8,128)(2,1)} %get-tuple-element.8.y_ref, bf16[2,512,768]{2,1,0:T(8,128)(2,1)} %get-tuple-element.9.tg_ref, f32[8,768]{1,0:T(8,128)} %get-tuple-element.10.gq_ref, ...), custom_call_target="tpu_custom_call" | custom-call | tf_op jit(solution)/shard_map/unturn/pallas_call | solution.py:626

commit v3 on v2

--- a/solution.py
+++ b/solution.py
@@ -487,18 +487,15 @@
         c = slice(HALF * j, HALF * (j + 1))
         return n1_s[r, span, c] * g1[...][None, c] + b1[...][None, c] + dot(act_s[r, span], flat(wout_s, c))
 
-    def outer_first(r):
-        dz_s[r, :, 0:HALF] = outer(r, slice(None), 0)
-
     def back(r):
         spans = [slice(HALF * b, HALF * (b + 1)) for b in range(2)]
 
         def summed(b, _):
-            return [outer(r, spans[b], j) for j in (1, 2)]
+            return [outer(r, spans[b], j) for j in range(3)]
 
         def second_norm(b, last):
             span = spans[b]
-            z2 = jnp.concatenate([dz_s[r, span, 0:HALF], *last], axis=1)
+            z2 = jnp.concatenate(last, axis=1)
             z2 = z2 - mean(z2)
             r2 = lax.rsqrt(mean(z2 * z2) + 1e-5)
             n2 = z2 * r2
@@ -588,9 +585,8 @@
     works += [({wv_g}, functools.partial(heads, r)) for r in range(rows)]
     works += [({wo_g}, each_row(attended))]
     works += [({win_g + j}, functools.partial(inner, r, j)) for j in range(4) for r in range(rows)]
-    works += [({wout_g}, each_row(outer_first))]
     net.run(works)
-    net.need(wout_g + 1, wout_g + 2)
+    net.need(wout_g, wout_g + 1, wout_g + 2)
     each_row(back)()
     lax.fori_loop(0, rows * PAIRS // 2, heads_back, 0)
     each_row(grads)()

time: 115 us -> 114 us (level)
  no operation moved by 1% of the time
where the time goes in v3:
time: 114 us
  Pallas kernels  114 us (100%)
    pallas_call x1, Pallas kernels, run_layer(): pl.pallas_call(functools.partial(layer_kernel, remote), out_shape=[act, a...  109 us
    pallas_call x1, Pallas kernels, unturn(): pl.pallas_call(unturn_kernel, grid=(y.shape[0],), out_shape=[act, act, gr...  4.85 us

profile of v3, /device:TPU:0, one launch (start us, length us, event | category | flops | bytes accessed | tf_op | source)
XLA Modules:
  0.0 114.2 jit_solution(9876767033665281392)
XLA Ops:
  0.6 108.7 %layer.1 = (bf16[2,512,768]{2,1,0:T(8,128)(2,1)}, bf16[2,512,768]{2,1,0:T(8,128)(2,1)}, f32[8,768]{1,0:T(8,128)}, f32[8,768]{1,0:T(8,128)}) custom-call(s32[2,512]{1,0:T(2,128)} %seg_ref.3, bf16[8,768]{1,0:T(8,128)(2,1)} %up_q.1, bf16[8,768]{1,0:T(8,128)(2,1)} %up_v.1, f32[768]{0:T(1024)} %g1.1, f32[768]{0:T(1024)} %b1.1, f32[768]{0:T(1024)} %g2.1, f32[768]{0:T(1024)} %b2.1, ...), custom_call_target="tpu_custom_call" | custom-call | tf_op jit(solution)/shard_map/layer/pallas_call | solution.py:666
  109.4 4.9 %unturn.1 = (bf16[2,512,768]{2,1,0:T(8,128)(2,1)}, bf16[2,512,768]{2,1,0:T(8,128)(2,1)}, f32[8,768]{1,0:T(8,128)}, f32[8,768]{1,0:T(8,128)}) custom-call(s32[2,512]{1,0:T(2,128)} %seg_ref.3, bf16[2,512,768]{2,1,0:T(8,128)(2,1)} %get-tuple-element.8.y_ref, bf16[2,512,768]{2,1,0:T(8,128)(2,1)} %get-tuple-element.9.tg_ref, f32[8,768]{1,0:T(8,128)} %get-tuple-element.10.gq_ref, ...), custom_call_target="tpu_custom_call" | custom-call | tf_op jit(solution)/shard_map/unturn/pallas_call | solution.py:622
